TPU v7x, 256 devices: a whole 4x4x8 slice. The times are simulated.
256 devices in a mesh: tgt: 32 (over y, x, z_lo), src: 8 (over z_hi, core).
Axes of the slice: x: 4, y: 4, z: 8 (z_hi: 4, z_lo: 2; z = z_hi * 2 + z_lo), core: 2. Of those that a mesh axis runs over, the one named last changes fastest.
Arguments:
- connectome: bfloat16 [4096, 51200], P('tgt', 'src'), may hold values from -0.02734375 to 0.02734375
- history: bfloat16 [32, 32, 51200], P('tgt', None, 'src'), may hold values from 0 to 5
- delays: int32 [32, 400], P('tgt', 'src'), may hold values from 16 to 32
- cycle_head: int32 [1], replicated, may hold values from 0 to 31
- outside_afferent: float32 [32], replicated, may hold values from 120 to 320
- init_state: float32 [6, 32, 4096], P(None, None, 'tgt'), may hold values from -4 to 4
- lead_field: bfloat16 [4096, 256], P('tgt'), may hold values from -0.09375 to 0.09375
Outputs:
- sensor_signal: float32 [32, 16, 256], P('tgt')
- final_state: float32 [6, 32, 4096], P(None, None, ('tgt', 'src'))
Inputs may be any that keep to these rules, and one draw needn't show every extreme that they name: `cycle_head`: a slot of the history cycle.
All inputs are finite; a program needn't handle non-finite values.
Results may differ from a plain program's by a relative error of at most 0.003.
Values may be sent and summed in bfloat16 or wider, within the bound.
No kernel may reach another device: no remote copies, remote signals or barrier semaphores. Data moves between devices by JAX's collectives and lax.ppermute only.
A program may use at most 128 MiB of HBM per device.

v0:
```python
import jax
import jax.numpy as jnp
from jax import lax
from jax.sharding import PartitionSpec as P

STEPS = 16
integrator_step_width = 0.1
positive_synaptic_amplitude = 0.0325
negative_synaptic_amplitude = 0.11
interneuron_fraction = 0.5
global_link_scale = 30.0
stellate_contact_count = 135.0
recurrent_loop_contacts = 108.0
interneuron_contact_count = 33.75
peak_spike_rate = 5.0
logistic_slope_factor = 0.56
logistic_midpoint = 6.0


def spike_rate_response(cell_depolarization):
    return peak_spike_rate * jax.nn.sigmoid(
        logistic_slope_factor * (cell_depolarization - logistic_midpoint)
    )


def advance(carry, applied_stimulus, outside_afferent):
    (
        principal_cell_depolarization,
        stellate_mean_depolarization,
        interneuron_mean_depolarization,
        principal_cell_slope,
        excite_rate,
        interneuron_slope,
    ) = carry
    next_principal_cell_slope = principal_cell_slope + integrator_step_width * (
        positive_synaptic_amplitude
        * spike_rate_response(stellate_mean_depolarization - interneuron_mean_depolarization)
        - 2.0 * principal_cell_slope
        - principal_cell_depolarization
    )
    summed_afferent_rate = (
        outside_afferent[:, None]
        + recurrent_loop_contacts
        * spike_rate_response(stellate_contact_count * principal_cell_depolarization)
        + global_link_scale * applied_stimulus
    )
    new_excite_rate = excite_rate + integrator_step_width * (
        positive_synaptic_amplitude * summed_afferent_rate
        - 2.0 * excite_rate
        - stellate_mean_depolarization
    )
    next_interneuron_slope = interneuron_slope + integrator_step_width * (
        negative_synaptic_amplitude
        * interneuron_contact_count
        * spike_rate_response(interneuron_contact_count * principal_cell_depolarization)
        - 2.0 * interneuron_fraction * interneuron_slope
        - interneuron_fraction * interneuron_fraction * interneuron_mean_depolarization
    )
    return (
        principal_cell_depolarization + integrator_step_width * principal_cell_slope,
        stellate_mean_depolarization + integrator_step_width * excite_rate,
        interneuron_mean_depolarization + integrator_step_width * interneuron_slope,
        next_principal_cell_slope,
        new_excite_rate,
        next_interneuron_slope,
    )


def integrate(init_state, outside_afferent, coupling):

    def one_step(carry, applied_stimulus):
        fresh = advance(carry, applied_stimulus, outside_afferent)
        return (fresh, fresh[1] - fresh[2])

    begin = tuple((init_state[member] for member in range(6)))
    final, potentials = lax.scan(one_step, begin, coupling)
    return (jnp.stack(final), potentials)


def body(connectome, history, delays, cycle_head, outside_afferent, init_state, lead_field):
    tgt_rows = connectome.shape[0]
    target_blocks = delays.shape[0]
    source_blocks = delays.shape[1]
    block_rows = tgt_rows // target_blocks
    block_cols = connectome.shape[1] // source_blocks
    members = history.shape[1]
    slots_all = history.shape[0] * lax.axis_size("tgt")
    tiles = connectome.reshape(target_blocks, block_rows, source_blocks, block_cols)
    moments = jnp.arange(STEPS, dtype=jnp.int32)
    lag_slot = (cycle_head[0] + moments[None, None, :] - delays[:, :, None]) % slots_all
    whole = lax.all_gather(history, "tgt", axis=0, tiled=True)
    stacked = whole.reshape(slots_all, members, source_blocks, block_cols)
    slot_ids = jnp.arange(slots_all, dtype=jnp.int32)
    wanted = lag_slot[0].T
    picker = (wanted[:, None, :] == slot_ids[None, :, None]).astype(jnp.bfloat16)
    window = jnp.einsum(
        "tkb,kmbs->tmbs", picker, stacked, preferred_element_type=jnp.float32
    ).astype(jnp.bfloat16)
    pieces = jnp.einsum("rbs,tmbs->tmr", tiles[0], window, preferred_element_type=jnp.float32)
    share = tgt_rows // lax.axis_size("src")
    offset_rows = lax.axis_index("src") * share
    summed = lax.psum(pieces, "src")
    final_full, potentials = integrate(init_state, outside_afferent, summed)
    final_state = lax.dynamic_slice_in_dim(final_full, offset_rows, share, 2)
    potential = potentials.astype(jnp.bfloat16)
    signal = lax.psum_scatter(
        jnp.einsum("tmr,rs->mts", potential, lead_field, preferred_element_type=jnp.float32),
        "tgt",
        scatter_dimension=0,
        tiled=True,
    )
    return (signal, final_state)


def solution(mesh):
    in_specs = (
        P("tgt", "src"),
        P("tgt", None, "src"),
        P("tgt", "src"),
        P(),
        P(),
        P(None, None, "tgt"),
        P("tgt", None),
    )
    out_specs = (P("tgt", None, None), P(None, None, ("tgt", "src")))
    return jax.shard_map(body, mesh=mesh, in_specs=in_specs, out_specs=out_specs, check_vma=False)
```

profile of v0, /device:TPU:64, one launch (start us, length us, event | category | flops | bytes accessed | tf_op | source)
XLA Modules:
  0.0 601.3 jit_solution(12034502340109940469)
XLA Ops:
  8.0 2.9 copy.27
  12.3 290.1 %all-gather.2.cloned.1.call-done = bf16[32,32,6400]{2,1,0:T(8,128)(2,1)} async-done(((bf16[1,32,6400]{2,1,0:T(8,128)(2,1)}), bf16[32,32,6400]{2,1,0:T(8,128)(2,1)}) %all-gather.2.cloned.1.call-update) | async-done | bytes 13107216 | tf_op jit(solution)/shard_map/all_gather | solution.py:91
  302.3 21.3 %reshape.45 = bf16[32,32,50,128]{3,2,1,0:T(8,128)(2,1)} reshape(bf16[32,32,6400]{2,1,0:T(8,128)(2,1)} %all-gather.2.cloned.1.call-done) | data formatting | bytes 26214400 | tf_op jit(solution)/shard_map/reshape | solution.py:92
  323.6 23.8 %fusion.10 = f32[16,32,128,1]{2,0,1,3:T(8,128)S(1)} fusion(bf16[128,50,128,1]{0,2,3,1:T(8,128)(2,1)S(1)} %bitcast.67, bf16[32,32,50,128]{3,2,1,0:T(8,128)(2,1)} %reshape.45, s32[16,50]{0,1:T(8,128)S(1)} %add_select_fusion), kind=kOutput, calls=%fused_computation.15 | convolution fusion | flops 1051878400 | bytes 15010944 | tf_op jit(solution)/shard_map/rbs,tmbs->tmr/dot_general | solution.py:99
  348.3 67.0 %all-reduce.2.cloned.1.call-done = f32[16,32,128]{2,1,0:T(8,128)} async-done(((f32[16,32,128]{2,1,0:T(8,128)}), f32[16,32,128]{2,1,0:T(8,128)}) %all-reduce.2.cloned.1.call-update) | async-done | bytes 262160 | tf_op jit(solution)/shard_map/psum | solution.py:102
  415.3 13.6 %while.25 = (s32[]{:T(128)}, f32[32,128]{1,0:T(8,128)S(1)}, f32[32,128]{1,0:T(8,128)S(1)}, f32[32,128]{1,0:T(8,128)S(1)}, f32[32,128]{1,0:T(8,128)S(1)}, /*index...) while((s32[]{:T(128)}, f32[32,128]{1,0:T(8,128)S(1)}, ...), condition=%wide.region_2.3_spmd, body=%wide.region_1.2_spmd.sunk | while | flops 192514 | bytes 360693 | solution.py:76
  415.3 0.8 multiply_add_fusion.8
  416.2 0.8 multiply_add_fusion.8
  417.0 0.8 multiply_add_fusion.8
  417.9 0.8 multiply_add_fusion.8
  418.7 0.8 multiply_add_fusion.8
  419.6 0.8 multiply_add_fusion.8
  420.4 0.8 multiply_add_fusion.8
  421.3 0.8 multiply_add_fusion.8
  422.1 0.8 multiply_add_fusion.8
  423.0 0.8 multiply_add_fusion.8
  423.8 0.8 multiply_add_fusion.8
  424.7 0.8 multiply_add_fusion.8
  425.5 0.8 multiply_add_fusion.8
  426.4 0.8 multiply_add_fusion.8
  427.2 0.8 multiply_add_fusion.8
  428.1 0.8 multiply_add_fusion.8
  429.2 1.1 copy.30
  431.2 163.6 %reduce-scatter.2.cloned.1.call-done = f32[1,16,256]{2,1,0:T(8,128)} async-done(((f32[32,16,256]{2,1,0:T(8,128)}), f32[1,16,256]{2,1,0:T(8,128)}) %reduce-scatter.2.cloned.1.call-update) | async-done | bytes 16400 | tf_op jit(solution)/shard_map/reduce_scatter | solution.py:106
  (74 shorter events, 3.8 us)
Async XLA Ops:
  7.2 421.8 %copy-start = (bf16[128,256]{1,0:T(8,128)(2,1)S(1)}, bf16[128,256]{1,0:T(8,128)(2,1)}, u32[]{:S(2)}) copy-start(bf16[128,256]{1,0:T(8,128)(2,1)} %param.15) | copy-start | bytes 196612
  7.2 295.2 %all-gather.2.cloned.1.call-start = ((), (), s32[]{:S(2)}) async-start(), calls=%async_computation.1 | async-start | bytes 13516800 | tf_op jit(solution)/shard_map/all_gather | solution.py:91
  7.9 407.4 %all-reduce.2.cloned.1.call-start = ((), (), s32[]{:S(2)}) async-start(), calls=%async_computation.2 | async-start | bytes 524288 | tf_op jit(solution)/shard_map/psum | solution.py:102
  323.6 24.7 %copy-start.1 = (f32[6,32,128]{2,1,0:T(8,128)S(1)}, f32[6,32,128]{2,1,0:T(8,128)}, u32[]{:S(2)}) copy-start(f32[6,32,128]{2,1,0:T(8,128)} %param.14) | copy-start | bytes 294916
  323.6 91.7 %copy-start.2 = (f32[32]{0:T(128)S(1)}, f32[32]{0:T(128)}, u32[]{:S(2)}) copy-start(f32[32]{0:T(128)} %param.13) | copy-start | bytes 388
  348.2 246.6 %reduce-scatter.2.cloned.1.call-start = ((), (), s32[]{:S(2)}) async-start(), calls=%async_computation.3 | async-start | bytes 540672 | tf_op jit(solution)/shard_map/reduce_scatter | solution.py:106
Sparse Core Ops, SparseCore 0:
  9.8 292.4 all-gather.1
  348.3 66.9 all-reduce.1
  430.4 164.3 reduce-scatter.1
where the time goes:
time: 603 us; the launch traced here: 601 us
  waiting for transfers between devices  521 us (86%)
  local copies, waits for them, and re-layouts  27 us (4%)
  matrix products  24 us (4%)
  between operations  14.5 us (2%)
  other arithmetic  13.7 us (2%)
    all_gather x1, waiting for transfers between devices, body(): whole = lax.all_gather(history, 'tgt', axis=0, tiled=True)  290 us
    reduce_scatter x1, waiting for transfers between devices, body(): lax.psum_scatter(jnp.einsum('tmr,rs->mts', potential, lead_field, preferr...  164 us
    psum x1, waiting for transfers between devices, body(): summed = lax.psum(pieces, 'src')  67 us
    dot_general x1, matrix products, body(): jnp.einsum('rbs,tmbs->tmr', tiles[0], window, preferred_element_type=jnp....  23.8 us
    reshape x1, local copies, waits for them, and re-layouts, body(): stacked = whole.reshape(slots_all, members, source_blocks, block_cols)  21.3 us
    add x16, other arithmetic, advance(): interneuron_slope + integrator_step_width * (negative_synaptic_amplitude...  12.7 us
  transfers between devices with their start and end apart: 3, of which 3 were waited for; matrix products, arithmetic and copies ran while one was open for 1% of the time, Pallas kernels for 0%

commit v1 on v0

--- a/solution.py
+++ b/solution.py
@@ -88,7 +88,9 @@
     tiles = connectome.reshape(target_blocks, block_rows, source_blocks, block_cols)
     moments = jnp.arange(STEPS, dtype=jnp.int32)
     lag_slot = (cycle_head[0] + moments[None, None, :] - delays[:, :, None]) % slots_all
-    whole = lax.all_gather(history, "tgt", axis=0, tiled=True)
+    built = jnp.stack([history for _ in range(lax.axis_size("tgt"))])
+    carry_in = lax.all_to_all(built, "tgt", 0, 0)
+    whole = jnp.concatenate(carry_in, axis=0)
     stacked = whole.reshape(slots_all, members, source_blocks, block_cols)
     slot_ids = jnp.arange(slots_all, dtype=jnp.int32)
     wanted = lag_slot[0].T

time: 603 us -> 545 us (0.904)
  waiting for transfers between devices: 521 us -> 449 us
  starting transfers between devices: 0.12 us -> 9 us
    all_gather x1 -> x0, waiting for transfers between devices: 290 us -> none  [body(): whole = lax.all_gather(history, 'tgt', axis=0, tiled=True)]
    all_to_all x0 -> x1, waiting for transfers between devices: none -> 190 us  [body(): carry_in = lax.all_to_all(built, 'tgt', 0, 0)]
    psum x1, waiting for transfers between devices: 67 us -> 95.6 us  [body(): summed = lax.psum(pieces, 'src')]
    another operation x0 -> x2, local copies, waits for them, and re-layouts: none -> 28.5 us  [the longest x1 21.3 us: body(): stacked = whole.reshape(slots_all, members, source_blocks, block_cols)]
    reshape x1 -> x0, local copies, waits for them, and re-layouts: 21.3 us -> none  [body(): stacked = whole.reshape(slots_all, members, source_blocks, block_cols)]
    all_to_all x0 -> x1, starting transfers between devices: none -> 8.92 us  [body(): carry_in = lax.all_to_all(built, 'tgt', 0, 0)]
  transfers between devices with their start and end apart: 3 -> 3, of which waited for: 3 -> 3; matrix products, arithmetic and copies ran while one was open for 1% -> 0% of each run, Pallas kernels for 0% -> 0%
where the time goes in v1:
time: 545 us; the launch traced here: 543 us
  waiting for transfers between devices  449 us (82%)
  local copies, waits for them, and re-layouts  32.8 us (6%)
  matrix products  24 us (4%)
  between operations  14.9 us (3%)
  other arithmetic  13.1 us (2%)
  starting transfers between devices  9 us (2%)
    all_to_all x1, waiting for transfers between devices, body(): carry_in = lax.all_to_all(built, 'tgt', 0, 0)  190 us
    reduce_scatter x1, waiting for transfers between devices, body(): lax.psum_scatter(jnp.einsum('tmr,rs->mts', potential, lead_field, preferr...  163 us
    psum x1, waiting for transfers between devices, body(): summed = lax.psum(pieces, 'src')  95.6 us
    dot_general x1, matrix products, body(): jnp.einsum('rbs,tmbs->tmr', tiles[0], window, preferred_element_type=jnp....  23.8 us
    another operation x1, local copies, waits for them, and re-layouts, body(): stacked = whole.reshape(slots_all, members, source_blocks, block_cols)  21.3 us
    add x16, other arithmetic, advance(): interneuron_slope + integrator_step_width * (negative_synaptic_amplitude...  12.7 us
  transfers between devices with their start and end apart: 3, of which 3 were waited for; matrix products, arithmetic and copies ran while one was open for 0% of the time, Pallas kernels for 0%

profile of v1, /device:TPU:64, one launch (start us, length us, event | category | flops | bytes accessed | tf_op | source)
XLA Modules:
  0.0 542.9 jit_solution(8627449223464097939)
XLA Ops:
  7.2 7.2 %stack.16 = bf16[32,1,32,6400]{3,2,1,0:T(8,128)(2,1)} broadcast(bf16[32,6400]{1,0:T(8,128)(2,1)} %bitcast.72), dimensions={2,3} | broadcast | bytes 13516800 | tf_op jit(solution)/shard_map/stack | solution.py:91
  14.4 8.9 %all-to-all-start = ((bf16[32,1,32,6400]{3,2,1,0:T(8,128)(2,1)}), bf16[32,1,32,6400]{3,2,1,0:T(8,128)(2,1)}, u32[]{:S(2)}, u32[]{:S(2)}) async-start(bf16[32,1,32,6400]{3,2,1,0:T(8,128)(2,1)} %stack.16), calls=%async_computation | async-start | bytes 26214400 | tf_op jit(solution)/shard_map/all_to_all | solution.py:92
  23.4 1.5 copy.27
  25.6 189.7 %all-to-all-done = bf16[32,1,32,6400]{3,2,1,0:T(8,128)(2,1)} async-done(((bf16[32,1,32,6400]{3,2,1,0:T(8,128)(2,1)}), bf16[32,1,32,6400]{3,2,1,0:T(8,128)(2,1)}, u32[]{:S(2)}, u32[]{:S(2)}) %all-to-all-start) | async-done | bytes 13107232 | tf_op jit(solution)/shard_map/all_to_all | solution.py:92
  215.3 21.3 %reshape_reshape.3 = bf16[32,32,50,128]{3,2,1,0:T(8,128)(2,1)} reshape(bf16[32,1,32,6400]{3,2,1,0:T(8,128)(2,1)} %all-to-all-done) | data formatting | bytes 26214400 | tf_op jit(solution)/shard_map/reshape;reshape | solution.py:94
  236.6 23.8 %fusion.10 = f32[16,32,128,1]{2,0,1,3:T(8,128)S(1)} fusion(bf16[128,50,128,1]{0,2,3,1:T(8,128)(2,1)S(1)} %bitcast.70, bf16[32,32,50,128]{3,2,1,0:T(8,128)(2,1)} %reshape_reshape.3, s32[16,50]{0,1:T(8,128)S(1)} %add_select_fusion), kind=kOutput, calls=%fused_computation.15 | convolution fusion | flops 1051878400 | bytes 15010944 | tf_op jit(solution)/shard_map/rbs,tmbs->tmr/dot_general | solution.py:101
  261.3 95.6 %all-reduce.2.cloned.1.call-done = f32[16,32,128]{2,1,0:T(8,128)} async-done(((f32[16,32,128]{2,1,0:T(8,128)}), f32[16,32,128]{2,1,0:T(8,128)}) %all-reduce.2.cloned.1.call-update) | async-done | bytes 262160 | tf_op jit(solution)/shard_map/psum | solution.py:104
  356.9 13.6 %while.25 = (s32[]{:T(128)}, f32[32,128]{1,0:T(8,128)S(1)}, f32[32,128]{1,0:T(8,128)S(1)}, f32[32,128]{1,0:T(8,128)S(1)}, f32[32,128]{1,0:T(8,128)S(1)}, /*index...) while((s32[]{:T(128)}, f32[32,128]{1,0:T(8,128)S(1)}, ...), condition=%wide.region_2.3_spmd, body=%wide.region_1.2_spmd.sunk | while | flops 192514 | bytes 360693 | solution.py:76
  357.8 0.8 multiply_add_fusion.8
  358.6 0.8 multiply_add_fusion.8
  359.5 0.8 multiply_add_fusion.8
  360.3 0.8 multiply_add_fusion.8
  361.2 0.8 multiply_add_fusion.8
  362.0 0.8 multiply_add_fusion.8
  362.9 0.8 multiply_add_fusion.8
  363.7 0.8 multiply_add_fusion.8
  364.6 0.8 multiply_add_fusion.8
  365.4 0.8 multiply_add_fusion.8
  366.3 0.8 multiply_add_fusion.8
  367.1 0.8 multiply_add_fusion.8
  368.0 0.8 multiply_add_fusion.8
  369.7 0.8 multiply_add_fusion.8
  370.8 1.1 copy.30
  372.8 163.3 %reduce-scatter.2.cloned.1.call-done = f32[1,16,256]{2,1,0:T(8,128)} async-done(((f32[32,16,256]{2,1,0:T(8,128)}), f32[1,16,256]{2,1,0:T(8,128)}) %reduce-scatter.2.cloned.1.call-update) | async-done | bytes 16400 | tf_op jit(solution)/shard_map/reduce_scatter | solution.py:108
  (78 shorter events, 4.0 us)
Async XLA Ops:
  7.2 363.4 %copy-start = (bf16[128,256]{1,0:T(8,128)(2,1)S(1)}, bf16[128,256]{1,0:T(8,128)(2,1)}, u32[]{:S(2)}) copy-start(bf16[128,256]{1,0:T(8,128)(2,1)} %param.15) | copy-start | bytes 196612
  14.4 9.0 %copy-start.1 = (bf16[128,6400]{1,0:T(8,128)(2,1)S(1)}, bf16[128,6400]{1,0:T(8,128)(2,1)}, u32[]{:S(2)}) copy-start(bf16[128,6400]{1,0:T(8,128)(2,1)} %param.9) | copy-start | bytes 4915204
  14.4 11.1 %copy-start.4 = (s32[1,50]{1,0:T(1,128)S(1)}, s32[1,50]{1,0:T(1,128)}, u32[]{:S(2)}) copy-start(s32[1,50]{1,0:T(1,128)} %param.11) | copy-start | bytes 604
  14.4 200.9 %all-to-all-start = ((bf16[32,1,32,6400]{3,2,1,0:T(8,128)(2,1)}), bf16[32,1,32,6400]{3,2,1,0:T(8,128)(2,1)}, u32[]{:S(2)}, u32[]{:S(2)}) async-start(bf16[32,1,32,6400]{3,2,1,0:T(8,128)(2,1)} %stack.16), calls=%async_computation | async-start | bytes 26214400 | tf_op jit(solution)/shard_map/all_to_all | solution.py:92
  23.3 333.6 %all-reduce.2.cloned.1.call-start = ((), (), s32[]{:S(2)}) async-start(), calls=%async_computation.2 | async-start | bytes 524288 | tf_op jit(solution)/shard_map/psum | solution.py:104
  236.6 24.7 %copy-start.2 = (f32[6,32,128]{2,1,0:T(8,128)S(1)}, f32[6,32,128]{2,1,0:T(8,128)}, u32[]{:S(2)}) copy-start(f32[6,32,128]{2,1,0:T(8,128)} %param.14) | copy-start | bytes 294916
  236.6 120.3 %copy-start.3 = (f32[32]{0:T(128)S(1)}, f32[32]{0:T(128)}, u32[]{:S(2)}) copy-start(f32[32]{0:T(128)} %param.13) | copy-start | bytes 388
  261.2 274.9 %reduce-scatter.2.cloned.1.call-start = ((), (), s32[]{:S(2)}) async-start(), calls=%async_computation.3 | async-start | bytes 540672 | tf_op jit(solution)/shard_map/reduce_scatter | solution.py:108
Sparse Core Ops, SparseCore 0:
  261.3 95.5 all-reduce.1
  372.0 163.9 reduce-scatter.1
